TPU v7x, 256 devices: a whole 4x4x8 slice. The times are simulated.
256 devices in a mesh: rep: 4 (over z_lo), fsdp: 64 (over x, z_hi, y, core).
Axes of the slice: x: 4, y: 4, z: 8 (z_hi: 2, z_lo: 4; z = z_hi * 4 + z_lo), core: 2. Of those that a mesh axis runs over, the one named last changes fastest.
Arguments:
- latents: bfloat16 [256, 16, 16, 640], P(('rep', 'fsdp')), may hold values from -6 to 6
- cotangent: bfloat16 [256, 16, 16, 640], P(('rep', 'fsdp')), may hold values from -6 to 6
- conv_weight: bfloat16 [4, 5760, 640], P('rep', 'fsdp'), may hold values from -0.078125 to 0.078125
- norm_gain: float32 [4, 640], P('rep'), may hold values from 0.5 to 1.5
- norm_shift: float32 [4, 640], P('rep'), may hold values from -3 to 3
- partner_bit: int32 [64], replicated, may hold values from 0 to 1
Outputs:
- block_out: bfloat16 [256, 16, 16, 640], P(('rep', 'fsdp'))
- input_grad: bfloat16 [256, 16, 16, 640], P(('rep', 'fsdp'))
- weight_grad: float32 [4, 5760, 640], P('rep', 'fsdp')
- norm_grad: float32 [4, 2, 640], P('rep')
Inputs may be any that keep to these rules, and one draw needn't show every extreme that they name: In row shard f, replica r is paired with replica r with bit partner_bit[f] of its index flipped.
All inputs are finite; a program needn't handle non-finite values.
Results may differ from a plain program's by a relative error of at most 0.0065.
Values may be sent and summed in bfloat16 or wider, within the bound.
A program may use at most 128 MiB of HBM per device.

v0:
```python
import jax
import jax.numpy as jnp
from jax import lax
from jax.sharding import PartitionSpec as P

GROUPS = 32


def partner(value, axis, stride):
    mask = 2**stride
    pairs = [(source, source ^ mask) for source in range(lax.axis_size(axis))]
    return lax.ppermute(value, axis, pairs)


def norm_forward(values_in, gain, shift, groups):
    count, side, chans = (values_in.shape[0], values_in.shape[1], values_in.shape[3])
    values = values_in.astype(jnp.float32).reshape(count, side * side, groups, chans // groups)
    center = jnp.mean(values, axis=(1, 3), keepdims=True)
    spread = jnp.mean(jnp.square(values - center), axis=(1, 3), keepdims=True)
    scale_inv = lax.rsqrt(spread + 1e-05)
    normed = (values - center) * scale_inv
    pre_act = normed * gain.reshape(groups, -1) + shift.reshape(groups, -1)
    return (normed, scale_inv, pre_act)


def make_patches(activation):
    count, side, chans = (activation.shape[0], activation.shape[1], activation.shape[3])
    padded = jnp.pad(activation, ((0, 0), (1, 1), (1, 1), (0, 0)))
    pieces = [
        padded[:, row_off : row_off + side, col_off : col_off + side, :]
        for row_off in range(3)
        for col_off in range(3)
    ]
    return jnp.concatenate(pieces, axis=-1).reshape(count * side * side, 9 * chans)


def fold_patches(patch_grad, count, side, chans):
    grads = patch_grad.reshape(count, side, side, 9, chans)
    total = jnp.zeros((count, side + 2, side + 2, chans), jnp.float32)
    for row_off in range(3):
        for col_off in range(3):
            tap = grads[:, :, :, row_off * 3 + col_off, :]
            total = total + jnp.pad(
                tap, ((0, 0), (row_off, 2 - row_off), (col_off, 2 - col_off), (0, 0))
            )
    return total[:, 1:-1, 1:-1, :]


def backward_rest(act_grad, normed, scale_inv, pre_act, gain, groups, inv_batch):
    count, side, chans = (act_grad.shape[0], act_grad.shape[1], act_grad.shape[3])
    act_grad = act_grad.reshape(count, side * side, groups, chans // groups)
    sigma = jax.nn.sigmoid(pre_act)
    pre_grad = act_grad * sigma * (1.0 + pre_act * (1.0 - sigma))
    gain_grad = jnp.sum(pre_grad * normed, axis=(0, 1)).reshape(-1) * inv_batch
    shift_grad = jnp.sum(pre_grad, axis=(0, 1)).reshape(-1) * inv_batch
    normed_grad = pre_grad * gain.reshape(groups, -1)
    first = jnp.mean(normed_grad, axis=(1, 3), keepdims=True)
    second = jnp.mean(normed_grad * normed, axis=(1, 3), keepdims=True)
    input_grad = scale_inv * (normed_grad - first - normed * second)
    return (
        input_grad.reshape(count, side, side, chans).astype(jnp.bfloat16),
        jnp.stack([gain_grad, shift_grad]),
    )


def shards(latents, cotangent, conv_weight, norm_gain, norm_shift, partner_bit):
    count, side, chans = (latents.shape[0], latents.shape[1], latents.shape[3])
    shard_total = lax.axis_size("fsdp")
    inv_batch = 1.0 / (count * shard_total)
    gain = norm_gain[0]
    normed, scale_inv, pre_act = norm_forward(latents, gain, norm_shift[0], GROUPS)
    activation = jax.nn.silu(pre_act).astype(jnp.bfloat16).reshape(count, side, side, chans)
    patches = make_patches(activation)
    cot_rows = cotangent.reshape(count * side * side, chans)
    weight_rows = conv_weight[0]
    output = jnp.dot(
        patches,
        lax.all_gather(weight_rows, "fsdp", axis=0, tiled=True),
        preferred_element_type=jnp.float32,
    )
    patch_grad = lax.dot_general(
        cot_rows,
        lax.all_gather(weight_rows, "fsdp", axis=0, tiled=True),
        (((1,), (1,)), ((), ())),
        preferred_element_type=jnp.float32,
    )
    block_out = output.astype(jnp.bfloat16).reshape(count, side, side, chans)
    act_grad = fold_patches(patch_grad, count, side, chans)
    input_grad, norm_term = backward_rest(
        act_grad, normed, scale_inv, pre_act, gain, GROUPS, inv_batch
    )
    weight_term = (
        lax.dot_general(
            patches, cot_rows, (((0,), (0,)), ((), ())), preferred_element_type=jnp.float32
        )
        * inv_batch
    )
    shard_rows = weight_rows.shape[0]
    term_pieces = weight_term.reshape(shard_total, shard_rows, chans)
    received = lax.all_to_all(
        term_pieces.astype(jnp.bfloat16), "fsdp", split_axis=0, concat_axis=0, tiled=True
    ).astype(term_pieces.dtype)
    weight_shard = jnp.sum(received, axis=0)
    bit_count = lax.axis_size("rep").bit_length() - 1
    shard_bit = lax.dynamic_index_in_dim(partner_bit, lax.axis_index("fsdp"), 0, keepdims=False)
    norm_bit = partner_bit[0]
    norm_total = lax.psum(norm_term, "fsdp")
    weight_avg, norm_avg = (weight_shard, norm_total)
    for bit_index in range(bit_count):
        other_weight, other_norm = (
            partner(weight_shard.astype(jnp.bfloat16), "rep", bit_index).astype(weight_shard.dtype),
            partner(norm_total.astype(jnp.bfloat16), "rep", bit_index).astype(norm_total.dtype),
        )
        weight_avg = jnp.where(
            shard_bit == bit_index, 0.5 * (weight_shard + other_weight), weight_avg
        )
        norm_avg = jnp.where(norm_bit == bit_index, 0.5 * (norm_total + other_norm), norm_avg)
    return (block_out, input_grad, weight_avg[None], norm_avg[None])


def solution(mesh):
    in_specs = (
        P(("rep", "fsdp"), None, None, None),
        P(("rep", "fsdp"), None, None, None),
        P("rep", "fsdp", None),
        P("rep", None),
        P("rep", None),
        P(),
    )
    out_specs = (
        P(("rep", "fsdp"), None, None, None),
        P(("rep", "fsdp"), None, None, None),
        P("rep", "fsdp", None),
        P("rep", None, None),
    )
    return jax.shard_map(shards, mesh=mesh, in_specs=in_specs, out_specs=out_specs, check_vma=False)
```

profile of v0, /device:TPU:0, one launch (start us, length us, event | category | flops | bytes accessed | tf_op | source)
XLA Modules:
  0.0 605.6 jit_solution(758910239517122541)
XLA Ops:
  7.2 1.8 copy.35
  9.1 1.0 convert_reduce_fusion.1
  10.2 0.1 reduce_sum.75
  10.5 1.1 fusion.28
  11.7 0.1 reduce_sum.96
  12.0 0.7 reduce.17
  12.7 0.7 reduce.18
  13.4 144.8 %all-gather.3.cloned.1.call-done = bf16[1,5760,640]{2,0,1:T(2,128)(2,1)} async-done(((bf16[1,90,640]{2,0,1:T(2,128)(2,1)}), bf16[1,5760,640]{2,0,1:T(2,128)(2,1)}) %all-gather.3.cloned.1.call-update) | async-done | bytes 7372816 | tf_op jit(solution)/shard_map/all_gather | solution.py:78
  158.2 9.4 %copy.45 = bf16[1,5760,640]{2,1,0:T(8,128)(2,1)} copy(bf16[1,5760,640]{2,0,1:T(2,128)(2,1)} %all-gather.3.cloned.1.call-done) | data formatting | bytes 14745600
  167.6 5.6 convolution_bitcast_fusion
  173.2 0.4 slice_bitcast_fusion.8
  173.7 0.2 pad_add_fusion
  173.9 0.8 copy-done.2
  174.6 0.9 fusion.27
  176.2 1.1 constant_dynamic-update-slice_fusion.9
  177.3 5.5 fusion
  182.8 9.1 %convert_element_type.71 = bf16[64,90,640]{2,1,0:T(8,128)(2,1)} reshape(bf16[5760,640]{1,0:T(8,128)(2,1)} %fusion) | data formatting | bytes 14745600 | tf_op jit(solution)/shard_map/convert_element_type | solution.py:101
  191.9 6.5 %all-to-all-start = ((bf16[64,90,640]{2,1,0:T(8,128)(2,1)}), bf16[64,90,640]{2,1,0:T(8,128)(2,1)}, u32[]{:S(2)}, u32[]{:S(2)}) async-start(bf16[64,90,640]{2,1,0:T(8,128)(2,1)} %convert_element_type.71), calls=%async_computation | async-start | bytes 15728640 | tf_op jit(solution)/shard_map/all_to_all | solution.py:100
  198.5 0.6 fusion.33
  201.7 354.6 %psum.7 = f32[2,640]{1,0:T(2,128)S(1)} all-reduce(f32[2,640]{1,0:T(2,128)S(1)} %pad_maximum_fusion), channel_id=1, replica_groups=mesh['rep'=4,'fsdp'=64] {'fsdp'}, use_global_device_ids=true, to_apply=%region_11.12 | all-reduce | flops 1280 | bytes 10240 | tf_op jit(solution)/shard_map/psum | solution.py:107
  556.3 9.9 %collective-permute-start.3 = (bf16[2,640]{1,0:T(2,128)(2,1)S(1)}, bf16[2,640]{1,0:T(2,128)(2,1)S(1)}, u32[]{:S(2)}, u32[]{:S(2)}) collective-permute-start(bf16[2,640]{1,0:T(2,128)(2,1)S(1)} %convert_element_type.76), channel_id=1, source_target_pairs={{0,64},{64,0},{128,192},{192,128},{1,65},{65,1},{129,193},{193,129... | collective-permute-start | bytes 7688 | tf_op jit(solution)/shard_map/ppermute | solution.py:12
  566.2 8.0 %collective-permute-start.2 = (bf16[2,640]{1,0:T(2,128)(2,1)S(1)}, bf16[2,640]{1,0:T(2,128)(2,1)S(1)}, u32[]{:S(2)}, u32[]{:S(2)}) collective-permute-start(bf16[2,640]{1,0:T(2,128)(2,1)S(1)} %convert_element_type.76), channel_id=1, source_target_pairs={{0,128},{64,192},{128,0},{192,64},{1,129},{65,193},{129,1},{193,65... | collective-permute-start | bytes 7688 | tf_op jit(solution)/shard_map/ppermute | solution.py:12
  575.0 1.0 constant_dynamic-update-slice_fusion.8
  576.0 1.0 constant_dynamic-update-slice_fusion.7
  577.4 0.9 fusion.26
  578.3 6.4 %fusion.4 = bf16[256,640]{1,0:T(8,128)(2,1)} fusion(bf16[256,5760]{1,0:T(8,128)(2,1)S(1)} %constant_dynamic-update-slice_fusion, bf16[1,5760,640]{2,1,0:T(8,128)(2,1)} %copy.45), kind=kOutput, calls=%fused_computation.7 | convolution fusion | flops 1887600640 | bytes 10649600 | tf_op jit(solution)/shard_map/dot_general | solution.py:76
  584.7 4.5 convert_reduce_fusion
  589.2 1.8 collective-permute-start.1
  591.0 0.6 select_bitcast_fusion
  591.6 2.5 collective-permute-done.1
  594.2 3.7 collective-permute-done
  597.9 0.8 broadcast_in_dim.4
  (55 shorter events, 2.4 us)
Async XLA Ops:
  7.2 160.5 %copy-start = (bf16[1,16,16,640]{3,2,1,0:T(8,128)(2,1)S(1)}, bf16[1,16,16,640]{3,2,1,0:T(8,128)(2,1)}, u32[]{:S(2)}) copy-start(bf16[1,16,16,640]{3,2,1,0:T(8,128)(2,1)} %param.7) | copy-start | bytes 983044
  7.2 151.0 %all-gather.3.cloned.1.call-start = ((), (), s32[]{:S(2)}) async-start(), calls=%async_computation.1 | async-start | bytes 14976000 | tf_op jit(solution)/shard_map/all_gather | solution.py:78
  173.7 1.0 copy-start.2
  191.9 6.5 %copy-start.4 = (s32[64]{0:T(128)S(1)}, s32[64]{0:T(128)}, u32[]{:S(2)}) copy-start(s32[64]{0:T(128)} %param.11) | copy-start | bytes 772
  191.9 385.1 %copy-start.3 = (bf16[1,16,16,640]{3,2,1,0:T(8,128)(2,1)S(1)}, bf16[1,16,16,640]{3,2,1,0:T(8,128)(2,1)}, u32[]{:S(2)}) copy-start(bf16[1,16,16,640]{3,2,1,0:T(8,128)(2,1)} %get-tuple-element.21) | copy-start | bytes 983044
  191.9 392.8 %all-to-all-start = ((bf16[64,90,640]{2,1,0:T(8,128)(2,1)}), bf16[64,90,640]{2,1,0:T(8,128)(2,1)}, u32[]{:S(2)}, u32[]{:S(2)}) async-start(bf16[64,90,640]{2,1,0:T(8,128)(2,1)} %convert_element_type.71), calls=%async_computation | async-start | bytes 15728640 | tf_op jit(solution)/shard_map/all_to_all | solution.py:100
  556.3 34.7 %collective-permute-start.3 = (bf16[2,640]{1,0:T(2,128)(2,1)S(1)}, bf16[2,640]{1,0:T(2,128)(2,1)S(1)}, u32[]{:S(2)}, u32[]{:S(2)}) collective-permute-start(bf16[2,640]{1,0:T(2,128)(2,1)S(1)} %convert_element_type.76), channel_id=1, source_target_pairs={{0,64},{64,0},{128,192},{192,128},{1,65},{65,1},{129,193},{193,129... | collective-permute-start | bytes 7688 | tf_op jit(solution)/shard_map/ppermute | solution.py:12
  566.2 24.9 %collective-permute-start.2 = (bf16[2,640]{1,0:T(2,128)(2,1)S(1)}, bf16[2,640]{1,0:T(2,128)(2,1)S(1)}, u32[]{:S(2)}, u32[]{:S(2)}) collective-permute-start(bf16[2,640]{1,0:T(2,128)(2,1)S(1)} %convert_element_type.76), channel_id=1, source_target_pairs={{0,128},{64,192},{128,0},{192,64},{1,129},{65,193},{129,1},{193,65... | collective-permute-start | bytes 7688 | tf_op jit(solution)/shard_map/ppermute | solution.py:12
  578.3 20.5 %copy-start.1 = (bf16[1,16,16,640]{3,2,1,0:T(8,128)(2,1)S(1)}, bf16[1,16,16,640]{3,2,1,0:T(8,128)(2,1)}, u32[]{:S(2)}) copy-start(bf16[1,16,16,640]{3,2,1,0:T(8,128)(2,1)} %param.7) | copy-start | bytes 983044
  589.2 5.0 collective-permute-start.1
  591.0 6.8 %collective-permute-start = (bf16[90,640]{1,0:T(8,128)(2,1)S(1)}, bf16[90,640]{1,0:T(8,128)(2,1)S(1)}, u32[]{:S(2)}, u32[]{:S(2)}) collective-permute-start(bf16[90,640]{1,0:T(8,128)(2,1)S(1)} %convert_element_type.73), channel_id=1, source_target_pairs={{0,128},{64,192},{128,0},{192,64},{1,129},{65,193},{129,1},{193,65... | collective-permute-start | bytes 345608 | tf_op jit(solution)/shard_map/ppermute | solution.py:12
Sparse Core Ops, SparseCore 0:
  12.1 146.0 all-gather.2
where the time goes:
time: 606 us
  blocking collectives  355 us (59%)
  waiting for transfers between devices  151 us (25%)
  local copies, waits for them, and re-layouts  28.1 us (5%)
  starting transfers between devices  26.3 us (4%)
  matrix products  17.5 us (3%)
  between operations  16.9 us (3%)
  other arithmetic  11.2 us (2%)
    psum x1, blocking collectives, shards(): norm_total = lax.psum(norm_term, 'fsdp')  355 us
    all_gather x1, waiting for transfers between devices, shards(): lax.all_gather(weight_rows, 'fsdp', axis=0, tiled=True)  145 us
    ppermute x4, starting transfers between devices, partner(): return lax.ppermute(value, axis, pairs)  19.7 us
    unnamed x28, local copies, waits for them, and re-layouts  14.9 us
  transfers between devices with their start and end apart: 6, of which 3 were waited for; matrix products, arithmetic and copies ran while one was open for 3% of the time, Pallas kernels for 0%

commit v1 on v0

--- a/solution.py
+++ b/solution.py
@@ -64,6 +64,16 @@
 
 
 def shards(latents, cotangent, conv_weight, norm_gain, norm_shift, partner_bit):
+
+    def wires_choose(vec, out_dim):
+        reply = jnp.concatenate(
+            jax.lax.all_to_all(
+                jnp.stack([vec] * jax.lax.axis_size("fsdp")), "fsdp", split_axis=0, concat_axis=0
+            ),
+            out_dim,
+        )
+        return reply
+
     count, side, chans = (latents.shape[0], latents.shape[1], latents.shape[3])
     shard_total = lax.axis_size("fsdp")
     inv_batch = 1.0 / (count * shard_total)
@@ -73,11 +83,7 @@
     patches = make_patches(activation)
     cot_rows = cotangent.reshape(count * side * side, chans)
     weight_rows = conv_weight[0]
-    output = jnp.dot(
-        patches,
-        lax.all_gather(weight_rows, "fsdp", axis=0, tiled=True),
-        preferred_element_type=jnp.float32,
-    )
+    output = jnp.dot(patches, wires_choose(weight_rows, 0), preferred_element_type=jnp.float32)
     patch_grad = lax.dot_general(
         cot_rows,
         lax.all_gather(weight_rows, "fsdp", axis=0, tiled=True),

time: 606 us -> 745 us (1.23)
  waiting for transfers between devices: 151 us -> 261 us
  blocking collectives: 355 us -> 370 us
  local copies, waits for them, and re-layouts: 28.1 us -> 41.3 us
    all_gather x1, waiting for transfers between devices: 145 us -> 258 us  [shards(): lax.all_gather(weight_rows, 'fsdp', axis=0, tiled=True)]
    psum x1, blocking collectives: 355 us -> 370 us  [shards(): norm_total = lax.psum(norm_term, 'fsdp')]
    ppermute x4, starting transfers between devices: 19.7 us -> 5.12 us  [partner(): return lax.ppermute(value, axis, pairs)]
    all_to_all x0 -> x1, starting transfers between devices: none -> 13.2 us  [wires_choose(): jax.lax.all_to_all(jnp.stack([vec] * jax.lax.axis_size('fsdp')), 'fsdp',...]
    reshape x0 -> x1, local copies, waits for them, and re-layouts: none -> 9.22 us  [wires_choose(): jnp.concatenate(jax.lax.all_to_all(jnp.stack([vec] * jax.lax.axis_size('f...]
  transfers between devices with their start and end apart: 6 -> 7, of which waited for: 3 -> 3; matrix products, arithmetic and copies ran while one was open for 3% -> 9% of each run, Pallas kernels for 0% -> 0%
where the time goes in v1:
time: 745 us; the launch traced here: 743 us
  blocking collectives  370 us (50%)
  waiting for transfers between devices  261 us (35%)
  local copies, waits for them, and re-layouts  41.3 us (6%)
  starting transfers between devices  28.4 us (4%)
  matrix products  17.5 us (2%)
  between operations  17 us (2%)
  other arithmetic  7.86 us (1%)
    psum x1, blocking collectives, shards(): norm_total = lax.psum(norm_term, 'fsdp')  370 us
    all_gather x1, waiting for transfers between devices, shards(): lax.all_gather(weight_rows, 'fsdp', axis=0, tiled=True)  258 us
  transfers between devices with their start and end apart: 7, of which 3 were waited for; matrix products, arithmetic and copies ran while one was open for 9% of the time, Pallas kernels for 0%

profile of v1, /device:TPU:0, one launch (start us, length us, event | category | flops | bytes accessed | tf_op | source)
XLA Modules:
  0.0 743.2 jit_solution(6781821197551256848)
XLA Ops:
  7.2 1.8 copy.35
  9.1 4.7 stack.8
  13.7 13.2 %all-to-all-start = ((bf16[64,90,640]{2,1,0:T(8,128)(2,1)}), bf16[64,90,640]{2,1,0:T(8,128)(2,1)}, u32[]{:S(2)}, u32[]{:S(2)}) async-start(bf16[64,90,640]{2,1,0:T(8,128)(2,1)} %stack.8), calls=%async_computation | async-start | bytes 15728640 | tf_op jit(solution)/shard_map/all_to_all | solution.py:70
  27.1 0.1 reduce_sum.75
  27.6 0.1 reduce_sum.96
  28.0 258.1 %all-gather.3.cloned.1.call-done = bf16[1,5760,640]{2,0,1:T(2,128)(2,1)} async-done(((bf16[1,90,640]{2,0,1:T(2,128)(2,1)}), bf16[1,5760,640]{2,0,1:T(2,128)(2,1)}) %all-gather.3.cloned.1.call-update) | async-done | bytes 7372816 | tf_op jit(solution)/shard_map/all_gather | solution.py:89
  286.1 9.5 %copy.45 = bf16[1,5760,640]{2,1,0:T(8,128)(2,1)} copy(bf16[1,5760,640]{2,0,1:T(2,128)(2,1)} %all-gather.3.cloned.1.call-done) | data formatting | bytes 14745600
  295.6 5.6 convolution_bitcast_fusion
  301.2 0.4 slice_bitcast_fusion.8
  301.6 0.2 pad_add_fusion
  301.8 0.9 fusion.22
  303.3 1.1 constant_dynamic-update-slice_fusion.9
  304.4 5.6 fusion
  310.0 9.1 %convert_element_type.71 = bf16[64,90,640]{2,1,0:T(8,128)(2,1)} reshape(bf16[5760,640]{1,0:T(8,128)(2,1)} %fusion) | data formatting | bytes 14745600 | tf_op jit(solution)/shard_map/convert_element_type | solution.py:107
  319.1 10.0 %all-to-all-start.1 = ((bf16[64,90,640]{2,1,0:T(8,128)(2,1)}), bf16[64,90,640]{2,1,0:T(8,128)(2,1)}, u32[]{:S(2)}, u32[]{:S(2)}) async-start(bf16[64,90,640]{2,1,0:T(8,128)(2,1)} %convert_element_type.71), calls=%async_computation.1 | async-start | bytes 15728640 | tf_op jit(solution)/shard_map/all_to_all | solution.py:106
  329.1 0.6 fusion.28
  332.4 369.9 %psum.7 = f32[2,640]{1,0:T(2,128)S(1)} all-reduce(f32[2,640]{1,0:T(2,128)S(1)} %pad_maximum_fusion), channel_id=1, replica_groups=mesh['rep'=4,'fsdp'=64] {'fsdp'}, use_global_device_ids=true, to_apply=%region_11.12 | all-reduce | flops 1280 | bytes 10240 | tf_op jit(solution)/shard_map/psum | solution.py:113
  702.4 1.2 collective-permute-start.3
  703.7 0.1 reduce_sum.102
  704.1 0.1 reduce_sum.99
  704.4 9.2 %reshape.219 = bf16[5760,640]{1,0:T(8,128)(2,1)} reshape(bf16[64,90,640]{2,1,0:T(8,128)(2,1)} %all-to-all-done) | data formatting | bytes 14745600 | tf_op jit(solution)/shard_map/reshape | solution.py:69
  713.6 1.0 constant_dynamic-update-slice_fusion.8
  714.7 1.0 constant_dynamic-update-slice_fusion.7
  716.0 0.9 fusion.21
  716.9 6.4 convolution_convert_fusion
  723.3 4.5 convert_reduce_fusion
  727.8 1.8 collective-permute-start
  729.6 2.0 collective-permute-start.1
  731.7 0.6 select_bitcast_fusion
  732.3 2.8 collective-permute-done
  735.1 0.3 collective-permute-done.1
  735.5 0.8 broadcast_in_dim.4
  (63 shorter events, 2.5 us)
Async XLA Ops:
  7.2 288.4 %copy-start = (bf16[1,16,16,640]{3,2,1,0:T(8,128)(2,1)S(1)}, bf16[1,16,16,640]{3,2,1,0:T(8,128)(2,1)}, u32[]{:S(2)}) copy-start(bf16[1,16,16,640]{3,2,1,0:T(8,128)(2,1)} %param.7) | copy-start | bytes 983044
  7.2 278.9 %all-gather.3.cloned.1.call-start = ((), (), s32[]{:S(2)}) async-start(), calls=%async_computation.2 | async-start | bytes 14976000 | tf_op jit(solution)/shard_map/all_gather | solution.py:89
  13.7 13.2 %copy-start.2 = (bf16[1,16,16,640]{3,2,1,0:T(8,128)(2,1)S(1)}, bf16[1,16,16,640]{3,2,1,0:T(8,128)(2,1)}, u32[]{:S(2)}) copy-start(bf16[1,16,16,640]{3,2,1,0:T(8,128)(2,1)} %param.6) | copy-start | bytes 983044
  13.7 14.2 %copy-start.4 = (f32[1,640]{1,0:T(1,128)S(1)}, f32[1,640]{1,0:T(1,128)}, u32[]{:S(2)}) copy-start(f32[1,640]{1,0:T(1,128)} %param.9) | copy-start | bytes 7684
  13.7 14.3 %copy-start.5 = (f32[1,640]{1,0:T(1,128)S(1)}, f32[1,640]{1,0:T(1,128)}, u32[]{:S(2)}) copy-start(f32[1,640]{1,0:T(1,128)} %param.10) | copy-start | bytes 7684
  13.7 305.3 %all-to-all-start = ((bf16[64,90,640]{2,1,0:T(8,128)(2,1)}), bf16[64,90,640]{2,1,0:T(8,128)(2,1)}, u32[]{:S(2)}, u32[]{:S(2)}) async-start(bf16[64,90,640]{2,1,0:T(8,128)(2,1)} %stack.8), calls=%async_computation | async-start | bytes 15728640 | tf_op jit(solution)/shard_map/all_to_all | solution.py:70
  319.1 10.0 %copy-start.6 = (s32[64]{0:T(128)S(1)}, s32[64]{0:T(128)}, u32[]{:S(2)}) copy-start(s32[64]{0:T(128)} %param.11) | copy-start | bytes 772
  319.1 404.2 %all-to-all-start.1 = ((bf16[64,90,640]{2,1,0:T(8,128)(2,1)}), bf16[64,90,640]{2,1,0:T(8,128)(2,1)}, u32[]{:S(2)}, u32[]{:S(2)}) async-start(bf16[64,90,640]{2,1,0:T(8,128)(2,1)} %convert_element_type.71), calls=%async_computation.1 | async-start | bytes 15728640 | tf_op jit(solution)/shard_map/all_to_all | solution.py:106
  702.3 29.4 %collective-permute-start.2 = (bf16[2,640]{1,0:T(2,128)(2,1)S(1)}, bf16[2,640]{1,0:T(2,128)(2,1)S(1)}, u32[]{:S(2)}, u32[]{:S(2)}) collective-permute-start(bf16[2,640]{1,0:T(2,128)(2,1)S(1)} %convert_element_type.76), channel_id=1, source_target_pairs={{0,128},{64,192},{128,0},{192,64},{1,129},{65,193},{129,1},{193,65... | collective-permute-start | bytes 7688 | tf_op jit(solution)/shard_map/ppermute | solution.py:12
  702.4 29.3 %collective-permute-start.3 = (bf16[2,640]{1,0:T(2,128)(2,1)S(1)}, bf16[2,640]{1,0:T(2,128)(2,1)S(1)}, u32[]{:S(2)}, u32[]{:S(2)}) collective-permute-start(bf16[2,640]{1,0:T(2,128)(2,1)S(1)} %convert_element_type.76), channel_id=1, source_target_pairs={{0,64},{64,0},{128,192},{192,128},{1,65},{65,1},{129,193},{193,129... | collective-permute-start | bytes 7688 | tf_op jit(solution)/shard_map/ppermute | solution.py:12
  704.4 11.3 %copy-start.3 = (bf16[1,16,16,640]{3,2,1,0:T(8,128)(2,1)S(1)}, bf16[1,16,16,640]{3,2,1,0:T(8,128)(2,1)}, u32[]{:S(2)}) copy-start(bf16[1,16,16,640]{3,2,1,0:T(8,128)(2,1)} %get-tuple-element.21) | copy-start | bytes 983044
  716.9 19.4 %copy-start.1 = (bf16[1,16,16,640]{3,2,1,0:T(8,128)(2,1)S(1)}, bf16[1,16,16,640]{3,2,1,0:T(8,128)(2,1)}, u32[]{:S(2)}) copy-start(bf16[1,16,16,640]{3,2,1,0:T(8,128)(2,1)} %param.7) | copy-start | bytes 983044
  727.8 7.3 collective-permute-start
  729.6 5.7 collective-permute-start.1
Sparse Core Ops, SparseCore 0:
  12.1 273.8 all-gather.2
